TPU v7x, 32 devices: a whole 2x2x4 slice. The times are simulated.
32 devices in a mesh: groups: 2 (over y), tm: 4 (over z), head: 2 (over x), batch: 2 (over core).
Axes of the slice: x: 2, y: 2, z: 4, core: 2. Of those that a mesh axis runs over, the one named last changes fastest.
Arguments:
- u_input: bfloat16 [4, 1024, 1536], P(('groups', 'batch'), 'tm'), parts along dimension 0, may hold values from -6 to 6
- head_values: bfloat16 [4, 1024, 3072], P(('groups', 'batch'), 'tm', 'head'), parts along dimension 0, may hold values from -6 to 6
- grad_output: bfloat16 [4, 1024, 3072], P(('groups', 'batch'), 'tm', 'head'), parts along dimension 0, may hold values from -6 to 6
- w_bc: bfloat16 [1536, 256], replicated, may hold values from -0.15625 to 0.15625
- w_dt: bfloat16 [1536, 48], P(None, 'head'), may hold values from -0.15625 to 0.15625
- dt_bias: float32 [48], P('head'), may hold values from -1.5 to 0.5
- a_log: float32 [48], P('head'), as said below
Outputs:
- grad_input: bfloat16 [4, 1024, 1536], P(('groups', 'batch'), 'tm'), parts along dimension 0
- grad_values: bfloat16 [4, 1024, 3072], P(('groups', 'batch'), 'tm', 'head'), parts along dimension 0
- grad_w_bc: float32 [3072, 256], P(('groups', 'tm', 'batch')), parts along dimension 0
- grad_w_dt: float32 [3072, 48], P('groups', 'head'), parts along dimension 0
- grad_dt_bias: float32 [96], P(('groups', 'head')), parts along dimension 0
- grad_a_log: float32 [96], P(('groups', 'head')), parts along dimension 0
There are 2 independent parts, one for each index of `groups`. A program takes and returns all parts, laid end to end along the dimension named above; an argument that names none is the same for every part. Nothing has to cross between parts.
Inputs may be any that keep to these rules, and one draw needn't show every extreme that they name: a_log lies between log(0.3 / 1024) and log(0.08).
All inputs are finite; a program needn't handle non-finite values.
Results may differ from a plain program's by a relative error of at most 0.0059.
Values may be sent and summed in bfloat16 or wider, within the bound.
A program may use at most 64 MiB of HBM per device.

v0:
```python
import jax
import jax.numpy as jnp
from jax import lax
from jax.sharding import PartitionSpec as P


def prefix(shard, axis, combine, identity, reverse):
    length, place = (lax.axis_size(axis), lax.axis_index(axis))
    everything = jax.tree.map(lambda part: lax.all_gather(part, axis), shard)
    start = jax.tree.map(
        lambda part, zero: jnp.broadcast_to(jnp.asarray(zero, part.dtype), part.shape),
        shard,
        identity,
    )

    def turn(k, before):
        at = length - 1 - k if reverse else k
        reached = at > place if reverse else at < place
        new = combine(before, jax.tree.map(lambda part: part[at], everything))
        return jax.tree.map(lambda a, b: jnp.where(reached, a, b), new, before)

    return lax.fori_loop(0, length, turn, start)


def span_core(b_rows, c_rows, time_step, values_in, rate, state_in):
    highest = lax.Precision.HIGHEST
    log_decay = jnp.cumsum(time_step * rate[None, :], axis=0)
    length_t = time_step.shape[0]
    causal = jnp.arange(length_t)[:, None] >= jnp.arange(length_t)[None, :]
    differ = log_decay.T[:, :, None] - log_decay.T[:, None, :]
    decay = jnp.exp(jnp.where(causal[None], differ, -jnp.inf))
    scores = jnp.dot(c_rows, b_rows.T, precision=highest)
    mixing = decay * scores[None] * time_step.T[:, None, :]
    inner = jnp.einsum("hts,shp->thp", mixing, values_in, precision=highest)
    carried = jnp.exp(log_decay)[:, :, None] * jnp.einsum(
        "tn,hpn->thp", c_rows, state_in, precision=highest
    )
    output = inner + carried
    tail_w = jnp.exp(log_decay[-1][None, :] - log_decay) * time_step
    final = jnp.exp(log_decay[-1])[:, None, None] * state_in + jnp.einsum(
        "sh,shp,sn->hpn", tail_w, values_in, b_rows, precision=highest
    )
    return (output, final)


def combine_maps(earlier, later):
    return (earlier[0] * later[0], later[0][..., None, None] * earlier[1] + later[1])


def on_device(u_input, head_values, grad_output, w_bc, w_dt, dt_bias, a_log):
    highest = lax.Precision.HIGHEST
    seq_count, token_count, width = u_input.shape
    heads = w_dt.shape[1]
    state_size = w_bc.shape[1] // 2
    head_size = head_values.shape[2] // heads
    rate = -jnp.exp(a_log)
    flat = u_input.reshape(seq_count * token_count, width)
    proj = jnp.dot(flat, w_bc, preferred_element_type=jnp.float32).astype(jnp.bfloat16)
    pre = jnp.dot(flat, w_dt, preferred_element_type=jnp.float32) + dt_bias[None, :]
    delta = jax.nn.softplus(pre).reshape(seq_count, token_count, heads)
    b_all = proj[:, :state_size].astype(jnp.float32).reshape(seq_count, token_count, state_size)
    c_all = proj[:, state_size:].astype(jnp.float32).reshape(seq_count, token_count, state_size)
    values_all = head_values.astype(jnp.float32).reshape(seq_count, token_count, heads, head_size)
    cotangent = grad_output.astype(jnp.float32).reshape(seq_count, token_count, heads, head_size)

    def summarize(b_rows, c_rows, time_step, values_in, grads_in):
        log_decay = jnp.cumsum(time_step * rate[None, :], axis=0)
        tail_w = jnp.exp(log_decay[-1][None, :] - log_decay) * time_step
        own_state = jnp.einsum("sh,shp,sn->hpn", tail_w, values_in, b_rows, precision=highest)
        pulled = jnp.einsum(
            "th,thp,tn->hpn", jnp.exp(log_decay), grads_in, c_rows, precision=highest
        )
        return (jnp.exp(log_decay[-1]), own_state, pulled)

    decays, own_states, pulls = jax.vmap(summarize)(b_all, c_all, delta, values_all, cotangent)
    unit = (jnp.ones_like(decays), jnp.zeros_like(own_states))
    incoming = prefix((decays, own_states), "tm", combine_maps, unit, False)[1]
    outgoing = prefix((decays, pulls), "tm", combine_maps, unit, True)[1]

    def backward_one(b_rows, c_rows, time_step, values_in, grads_in, state_in, state_grad):
        _, pull_back = jax.vjp(span_core, b_rows, c_rows, time_step, values_in, rate, state_in)
        return pull_back((grads_in, state_grad))

    g_b, g_c, g_delta, g_x, g_rate, _ = jax.vmap(backward_one)(
        b_all, c_all, delta, values_all, cotangent, incoming, outgoing
    )
    partial_proj = jnp.concatenate([g_b, g_c], axis=-1).reshape(
        seq_count * token_count, 2 * state_size
    )
    grad_proj = lax.psum(partial_proj, "head").astype(jnp.bfloat16)
    grad_pre = g_delta.reshape(seq_count * token_count, heads) * jax.nn.sigmoid(pre)
    grad_pre_b = grad_pre.astype(jnp.bfloat16)
    from_bc = jnp.dot(grad_proj, w_bc.T, preferred_element_type=jnp.float32)
    all_pre, all_w_dt = (
        lax.all_gather(grad_pre_b, "head", axis=1, tiled=True),
        lax.all_gather(w_dt, "head", axis=1, tiled=True),
    )
    grad_input = from_bc + jnp.dot(all_pre, all_w_dt.T, preferred_element_type=jnp.float32)
    grad_input = grad_input.astype(jnp.bfloat16).reshape(seq_count, token_count, width)
    grad_values = g_x.reshape(seq_count, token_count, heads * head_size).astype(jnp.bfloat16)
    local_w_dt = jnp.einsum("td,th->dh", flat, grad_pre_b, preferred_element_type=jnp.float32)
    grad_w_dt, grad_dt_bias, grad_a_log = lax.psum(
        (local_w_dt, jnp.sum(grad_pre, axis=0), jnp.sum(g_rate, axis=0) * rate), ("tm", "batch")
    )
    local_w_bc = jnp.einsum("td,tk->dk", flat, grad_proj, preferred_element_type=jnp.float32)
    grad_w_bc = lax.psum_scatter(local_w_bc, ("tm", "batch"), scatter_dimension=0, tiled=True)
    return (grad_input, grad_values, grad_w_bc, grad_w_dt, grad_dt_bias, grad_a_log)


def solution(mesh):
    return jax.shard_map(
        on_device,
        mesh=mesh,
        in_specs=(
            P(("groups", "batch"), "tm", None),
            P(("groups", "batch"), "tm", "head"),
            P(("groups", "batch"), "tm", "head"),
            P(),
            P(None, "head"),
            P("head"),
            P("head"),
        ),
        out_specs=(
            P(("groups", "batch"), "tm", None),
            P(("groups", "batch"), "tm", "head"),
            P(("groups", "tm", "batch"), None),
            P("groups", "head"),
            P(("groups", "head")),
            P(("groups", "head")),
        ),
        check_vma=False,
    )
```

profile of v0, /device:TPU:0, one launch (start us, length us, event | category | flops | bytes accessed | tf_op | source)
XLA Modules:
  0.0 287.1 jit_solution(3803811651553812673)
XLA Ops:
  7.2 0.8 exponential_negate_fusion
  8.3 1.2 convolution_add_fusion.1
  9.6 0.7 fusion.64
  10.4 0.6 reduce-window.14
  11.6 0.7 copy.87
  12.9 0.5 copy-done.16
  13.4 1.8 fusion.20
  15.3 1.4 copy.91
  16.7 12.8 %all_gather.24 = f32[4,1,24]{2,1,0:T(1,128)} all-gather(f32[1,1,24]{2,1,0:T(1,128)S(1)} %get-tuple-element.385), channel_id=1, replica_groups=mesh['groups'=2,'tm'=4,'head'=2,'batch'=2] {'tm'}, dimensions={0}, use_global_device_ids=true | all-gather | bytes 480 | tf_op jit(solution)/shard_map/all_gather | solution.py:9
  29.5 52.0 %all-gather.5.cloned.1.call-done = f32[96,64,128]{2,1,0:T(8,128)} async-done(((f32[24,64,128]{2,1,0:T(8,128)}), f32[96,64,128]{2,1,0:T(8,128)}) %all-gather.5.cloned.1.call-update) | async-done | bytes 3145744 | tf_op jit(solution)/shard_map/all_gather | solution.py:9
  81.6 7.8 %while.30 = (s32[]{:T(128)}, f32[1,24,64,128]{3,2,1,0:T(8,128)S(1)}, s32[]{:T(128)}, f32[4,1,24]{2,1,0:T(1,128)}, f32[4,1,24,64,128]{4,3,2,1,0:T(8,128)}, /*index=5*/s32[]{:T(128)}, s32[]{:T(128)}, s32[]{:T(128)}, s32[]{:T(128)}) while((s32[]{:T(128)}, f32[1,24,64,128]{3,2,1,0:T(8,128)S(1)}, s32[]{:T(128)}, f32[4,1,24]{2,1,0:T(1,128)}, ...), condition=%wide.region_3.4_spmd.clone, body=%wide.region_2.3_spmd.clone.sunk | while | flops 786440 | bytes 2359751 | solution.py:22
  81.6 0.7 dynamic-slice_bitcast_fusion.4
  82.2 1.3 fusion.85
  83.5 0.6 dynamic-slice_bitcast_fusion.4
  84.1 1.3 fusion.85
  85.5 0.6 dynamic-slice_bitcast_fusion.4
  86.1 1.3 fusion.85
  87.4 0.7 dynamic-slice_bitcast_fusion.4
  88.1 1.3 fusion.85
  89.4 2.5 fusion.18
  91.9 1.5 copy.111
  93.4 2.2 fusion.61
  95.6 1.6 copy.90
  97.2 2.5 fusion.16
  100.0 1.4 copy.92
  101.3 2.0 bitcast_multiply_fusion.1
  103.4 0.7 broadcast.77
  104.0 1.6 copy.112
  105.6 1.6 copy.95
  107.3 0.8 bitcast_add_fusion.8
  108.2 6.4 %fusion.7 = (f32[24,256]{1,0:T(8,128)}, f32[24,256]{1,0:T(8,128)}, f32[24,256]{1,0:T(8,128)}, f32[256,256]{1,0:T(8,128)}) fusion(f32[256,256]{1,0:T(8,128)S(1)} %fusion.53, f32[24,256]{1,0:T(8,128)} %copy.95, f32[24,256]{1,0:T(8,128)S(1)} %bitcast_add_fusion.8, pred[256,256]{1,0:T(8,128)(4,1)S(1)} %iota_compare_fusion, ...), kind=kOutput, calls=%fused_computation.14 | convolution fusion | flops 221689856 | bytes 2285568 | tf_op jit(solution)/shard_map/vmap(transpose(jvp(hts,shp->thp)))/dot_general | solution.py:34
  114.6 1.5 copy.100
  116.1 1.5 copy.99
  117.6 1.5 copy.97
  119.1 1.2 convolution_bitcast_fusion.3
  120.3 3.3 %fusion.25 = f32[1,256,128]{1,2,0:T(8,128)} fusion(f32[1,256,128]{1,2,0:T(8,128)S(1)} %convolution_bitcast_fusion.3, bf16[256,24,64]{0,2,1:T(8,128)(2,1)} %bitcast.249, f32[1,24,64,128]{3,2,1,0:T(8,128)S(1)} %get-tuple-element.232, f32[256,24]{0,1:T(8,128)} %copy.90), kind=kOutput, calls=%fused_computation.42 | convolution fusion | flops 604798976 | bytes 1859584 | tf_op jit(solution)/shard_map/vmap(transpose(jvp(sh,shp,sn->hpn)))/dot_general | solution.py:40
  123.6 38.5 %all-gather.7.cloned.1.call-done = f32[96,64,128]{2,1,0:T(8,128)} async-done(((f32[24,64,128]{2,1,0:T(8,128)}), f32[96,64,128]{2,1,0:T(8,128)}) %all-gather.7.cloned.1.call-update) | async-done | bytes 3145744 | tf_op jit(solution)/shard_map/all_gather | solution.py:9
  162.1 7.8 %while.31 = (s32[]{:T(128)}, f32[1,24,64,128]{3,2,1,0:T(8,128)S(1)}, s32[]{:T(128)}, f32[4,1,24]{2,1,0:T(1,128)}, f32[4,1,24,64,128]{4,3,2,1,0:T(8,128)}, /*index=5*/s32[]{:T(128)}, s32[]{:T(128)}) while((s32[]{:T(128)}, f32[1,24,64,128]{3,2,1,0:T(8,128)S(1)}, s32[]{:T(128)}, f32[4,1,24]{2,1,0:T(1,128)}, ...), condition=%wide.region_6.7_spmd.clone, body=%wide.region_5.6_spmd.clone.sunk | while | flops 786436 | bytes 2359689 | solution.py:22
  162.1 0.7 dynamic-slice_bitcast_fusion.5
  162.7 1.3 fusion.86
  164.1 0.6 dynamic-slice_bitcast_fusion.5
  164.7 1.3 fusion.86
  166.0 0.6 dynamic-slice_bitcast_fusion.5
  166.6 1.3 fusion.86
  167.9 0.7 dynamic-slice_bitcast_fusion.5
  168.6 1.3 fusion.86
  170.2 0.8 multiply_reduce_fusion.2
  171.4 2.5 reduce-window.16
  174.1 2.9 %convolution_bitcast_fusion.2 = f32[256,128]{0,1:T(8,128)S(1)} fusion(f32[256,24,64]{0,2,1:T(8,128)} %bitcast.250, f32[1,24,64,128]{3,2,1,0:T(8,128)S(1)} %get-tuple-element.233), kind=kOutput, calls=%fused_computation.40 | convolution fusion | flops 603979776 | bytes 2490368 | tf_op jit(solution)/shard_map/vmap(transpose(jvp(tn,hpn->thp)))/dot_general | solution.py:35
  177.4 11.5 %all-reduce.7 = bf16[256,256]{0,1:T(8,128)(2,1)S(1)} all-reduce(f32[256,256]{0,1:T(8,128)S(1)} %maximum_bitcast_fusion), channel_id=1, replica_groups=mesh['groups'=2,'tm'=4,'head'=2,'batch'=2] {'head'}, use_global_device_ids=true, to_apply=%region_7.8 | all-reduce | flops 65536 | bytes 393216 | tf_op jit(solution)/shard_map/psum | solution.py:90
  188.9 0.6 fusion.65
  189.5 0.9 convolution_bitcast_fusion.1
  190.5 1.5 convolution_bitcast_fusion
  192.0 3.0 %copy.113 = f32[1536,256]{1,0:T(8,128)} copy(f32[1536,256]{0,1:T(8,128)} %convolution_bitcast_fusion) | data formatting | bytes 3145728
  195.1 0.8 copy-done.12
  195.9 5.0 %all_gather.30 = bf16[1536,48]{0,1:T(8,128)(2,1)S(1)} all-gather(bf16[1536,24]{0,1:T(8,128)(2,1)S(1)} %copy-done.12), channel_id=1, replica_groups=mesh['groups'=2,'tm'=4,'head'=2,'batch'=2] {'head'}, dimensions={1}, use_global_device_ids=true | all-gather | bytes 221184 | tf_op jit(solution)/shard_map/all_gather | solution.py:96
  201.0 6.0 %fusion.19 = bf16[1,256,24,64]{1,3,2,0:T(8,128)(2,1)} fusion(f32[24,64,256]{2,1,0:T(8,128)} %get-tuple-element.387, bf16[24,64,256]{2,1,0:T(8,128)(2,1)S(1)} %bitcast.245, f32[256,256]{1,0:T(8,128)S(1)} %copy-done.14, f32[24,256]{1,0:T(8,128)S(1)} %copy-done.19, f32[24,256]{1,0:T(8,128)S(1)} %copy-done.21, pred[256,256]{1,0:T(8,128)(4,1)S(1)} %copy-done.18, ...), kind=kOutput, calls=%fused_computation.32 | convolution fusion | flops 1215430656 | bytes 3547136 | tf_op jit(solution)/shard_map/vmap(transpose(jvp(hts,shp->thp)))/dot_general | solution.py:34
  207.0 2.4 copy.104
  209.6 14.1 %all-reduce.2 = (f32[24]{0:T(128)}, f32[24]{0:T(128)}) all-reduce(f32[24]{0:T(128)S(1)} %copy-done.25, f32[24]{0:T(128)S(1)} %fusion.63), channel_id=1, replica_groups=mesh['groups'=2,'tm'=4,'head'=2,'batch'=2] {'tm','batch'}, use_global_device_ids=true, to_apply=%region_19.20 | all-reduce | flops 48 | bytes 384 | tf_op jit(solution)/shard_map/psum | solution.py:102
  223.7 4.4 %all_gather.29 = bf16[256,48]{0,1:T(8,128)(2,1)S(1)} all-gather(bf16[256,24]{0,1:T(8,128)(2,1)S(1)} %copy.103), channel_id=1, replica_groups=mesh['groups'=2,'tm'=4,'head'=2,'batch'=2] {'head'}, dimensions={1}, use_global_device_ids=true | all-gather | bytes 36864 | tf_op jit(solution)/shard_map/all_gather | solution.py:95
  228.5 1.3 fusion.15
  229.8 10.8 %all-reduce.6.cloned.1.call-done = f32[1536,24]{0,1:T(8,128)} async-done(((f32[1536,24]{0,1:T(8,128)}), f32[1536,24]{0,1:T(8,128)}) %all-reduce.6.cloned.1.call-update) | async-done | bytes 147472 | tf_op jit(solution)/shard_map/psum | solution.py:102
  240.6 38.4 %reduce-scatter.4.cloned.1.call-done = f32[192,256]{1,0:T(8,128)} async-done(((f32[1536,256]{1,0:T(8,128)}), f32[192,256]{1,0:T(8,128)}) %reduce-scatter.4.cloned.1.call-update) | async-done | bytes 196624
  279.0 1.6 copy.132
  (88 shorter events, 4.2 us)
Async XLA Ops:
  7.2 1.2 copy-start
  7.2 5.1 %copy-start.2 = (bf16[1536,256]{1,0:T(8,128)(2,1)S(1)}, bf16[1536,256]{1,0:T(8,128)(2,1)}, u32[]{:S(2)}) copy-start(bf16[1536,256]{1,0:T(8,128)(2,1)} %param.14) | copy-start | bytes 2359300
  7.2 74.4 %all-gather.5.cloned.1.call-start = ((), (), s32[]{:S(2)}) async-start(), calls=%async_computation.2 | async-start | bytes 3932160 | tf_op jit(solution)/shard_map/all_gather | solution.py:9
  9.5 3.1 %copy-start.6 = (bf16[1,256,1536]{2,1,0:T(8,128)(2,1)S(1)}, bf16[1,256,1536]{2,1,0:T(8,128)(2,1)}, u32[]{:S(2)}) copy-start(bf16[1,256,1536]{2,1,0:T(8,128)(2,1)} %param.13) | copy-start | bytes 2359300
  10.9 0.6 copy-start.11
  12.6 0.7 copy-start.16
  15.2 146.9 %all-gather.7.cloned.1.call-start = ((), (), s32[]{:S(2)}) async-start(), calls=%async_computation.3 | async-start | bytes 3932160 | tf_op jit(solution)/shard_map/all_gather | solution.py:9
  16.7 80.5 %copy-start.1 = (bf16[1,256,1536]{1,2,0:T(8,128)(2,1)}, bf16[1,256,1536]{1,2,0:T(8,128)(2,1)S(1)}, u32[]{:S(2)}) copy-start(bf16[1,256,1536]{1,2,0:T(8,128)(2,1)S(1)} %copy.91) | copy-start | bytes 2359300
  99.8 140.8 %all-reduce.6.cloned.1.call-start = ((), (), s32[]{:S(2)}) async-start(), calls=%async_computation.1 | async-start | bytes 294912 | tf_op jit(solution)/shard_map/psum | solution.py:102
  107.2 7.4 %copy-start.17 = (pred[256,256]{1,0:T(8,128)(4,1)}, pred[256,256]{1,0:T(8,128)(4,1)S(1)}, u32[]{:S(2)}) copy-start(pred[256,256]{1,0:T(8,128)(4,1)S(1)} %iota_compare_fusion) | copy-start | bytes 196612
  108.0 6.6 %copy-start.20 = (f32[24,256]{1,0:T(8,128)}, f32[24,256]{1,0:T(8,128)S(1)}, u32[]{:S(2)}) copy-start(f32[24,256]{1,0:T(8,128)S(1)} %bitcast_add_fusion.8) | copy-start | bytes 73732
  108.2 6.4 %copy-start.13 = (f32[256,256]{1,0:T(8,128)}, f32[256,256]{1,0:T(8,128)S(1)}, u32[]{:S(2)}) copy-start(f32[256,256]{1,0:T(8,128)S(1)} %fusion.53) | copy-start | bytes 786436
  169.9 1.2 copy-start.24
  170.2 0.9 copy-start.4
  170.2 1.0 copy-start.9
  170.2 1.0 copy-start.10
  171.3 5.7 %copy-start.5 = (f32[256,256]{1,0:T(8,128)S(1)}, f32[256,256]{1,0:T(8,128)}, u32[]{:S(2)}) copy-start(f32[256,256]{1,0:T(8,128)} %get-tuple-element.353) | copy-start | bytes 786436
  174.0 3.4 %copy-start.7 = (f32[1,256,128]{1,2,0:T(8,128)S(1)}, f32[1,256,128]{1,2,0:T(8,128)}, u32[]{:S(2)}) copy-start(f32[1,256,128]{1,2,0:T(8,128)} %fusion.25) | copy-start | bytes 393220
  174.1 14.8 %copy-start.22 = (f32[24,2]{0,1:T(2,128)}, f32[24,2]{0,1:T(2,128)S(1)}, u32[]{:S(2)}) copy-start(f32[24,2]{0,1:T(2,128)S(1)} %slice_bitcast_fusion) | copy-start | bytes 580
  174.1 14.8 %copy-start.8 = (f32[24,256]{0,1:T(8,128)S(1)}, f32[24,256]{0,1:T(8,128)}, u32[]{:S(2)}) copy-start(f32[24,256]{0,1:T(8,128)} %copy.97) | copy-start | bytes 73732
  190.4 88.6 %reduce-scatter.4.cloned.1.call-start = ((), (), s32[]{:S(2)}) async-start(), calls=%async_computation.4 | async-start | bytes 1769472
  195.0 0.9 copy-start.12
  195.1 5.9 %copy-start.14 = (f32[256,256]{1,0:T(8,128)S(1)}, f32[256,256]{1,0:T(8,128)}, u32[]{:S(2)}) copy-start(f32[256,256]{1,0:T(8,128)} %copy-done.13) | copy-start | bytes 786436
  195.1 5.9 %copy-start.15 = (f32[256,24]{0,1:T(8,128)S(1)}, f32[256,24]{0,1:T(8,128)}, u32[]{:S(2)}) copy-start(f32[256,24]{0,1:T(8,128)} %copy.90) | copy-start | bytes 73732
  195.1 5.9 %copy-start.18 = (pred[256,256]{1,0:T(8,128)(4,1)S(1)}, pred[256,256]{1,0:T(8,128)(4,1)}, u32[]{:S(2)}) copy-start(pred[256,256]{1,0:T(8,128)(4,1)} %copy-done.17) | copy-start | bytes 196612
  195.1 5.9 %copy-start.19 = (f32[24,256]{1,0:T(8,128)S(1)}, f32[24,256]{1,0:T(8,128)}, u32[]{:S(2)}) copy-start(f32[24,256]{1,0:T(8,128)} %copy.95) | copy-start | bytes 73732
  195.1 5.9 %copy-start.21 = (f32[24,256]{1,0:T(8,128)S(1)}, f32[24,256]{1,0:T(8,128)}, u32[]{:S(2)}) copy-start(f32[24,256]{1,0:T(8,128)} %copy-done.20) | copy-start | bytes 73732
  207.0 2.4 copy-start.23
  207.0 2.6 copy-start.26
  207.0 2.6 copy-start.25
  207.0 21.1 %copy-start.3 = (bf16[1536,256]{1,0:T(8,128)(2,1)S(1)}, bf16[1536,256]{1,0:T(8,128)(2,1)}, u32[]{:S(2)}) copy-start(bf16[1536,256]{1,0:T(8,128)(2,1)} %param.14) | copy-start | bytes 2359300
Sparse Core Ops, SparseCore 0:
  15.3 66.1 all-gather.4
  99.9 62.1 all-gather.6
  190.6 49.9 all-reduce.5
  243.4 35.5 reduce-scatter.3
where the time goes:
time: 289 us; the launch traced here: 287 us
  waiting for transfers between devices  140 us (48%)
  blocking collectives  47.8 us (17%)
  matrix products  33.6 us (12%)
  local copies, waits for them, and re-layouts  30 us (10%)
  other arithmetic  21.3 us (7%)
  between operations  14.1 us (5%)
    all_gather x2, waiting for transfers between devices, prefix(): everything = jax.tree.map(lambda part: lax.all_gather(part, axis), shard)  90.5 us
    unnamed x5, waiting for transfers between devices  38.5 us
    psum x1, blocking collectives, on_device(): lax.psum((local_w_dt, jnp.sum(grad_pre, axis=0), jnp.sum(g_rate, axis=0)...  14.1 us
    all_gather x1, blocking collectives, prefix(): everything = jax.tree.map(lambda part: lax.all_gather(part, axis), shard)  12.8 us
    dot_general x2, matrix products, span_core(): inner = jnp.einsum('hts,shp->thp', mixing, values_in, precision=highest)  12.4 us
    psum x1, blocking collectives, on_device(): grad_proj = lax.psum(partial_proj, 'head').astype(jnp.bfloat16)  11.5 us
    psum x1, waiting for transfers between devices, on_device(): lax.psum((local_w_dt, jnp.sum(grad_pre, axis=0), jnp.sum(g_rate, axis=0)...  10.8 us
    unnamed x59, local copies, waits for them, and re-layouts  10.7 us
  transfers between devices with their start and end apart: 4, of which 4 were waited for; matrix products, arithmetic and copies ran while one was open for 14% of the time, Pallas kernels for 0%

commit v1 on v0

--- a/solution.py
+++ b/solution.py
@@ -100,7 +100,8 @@
     grad_values = g_x.reshape(seq_count, token_count, heads * head_size).astype(jnp.bfloat16)
     local_w_dt = jnp.einsum("td,th->dh", flat, grad_pre_b, preferred_element_type=jnp.float32)
     grad_w_dt, grad_dt_bias, grad_a_log = lax.psum(
-        (local_w_dt, jnp.sum(grad_pre, axis=0), jnp.sum(g_rate, axis=0) * rate), ("tm", "batch")
+        lax.psum((local_w_dt, jnp.sum(grad_pre, axis=0), jnp.sum(g_rate, axis=0) * rate), "batch"),
+        "tm",
     )
     local_w_bc = jnp.einsum("td,tk->dk", flat, grad_proj, preferred_element_type=jnp.float32)
     grad_w_bc = lax.psum_scatter(local_w_bc, ("tm", "batch"), scatter_dimension=0, tiled=True)

time: 289 us -> 279 us (0.965)
  waiting for transfers between devices: 140 us -> 133 us
  local copies, waits for them, and re-layouts: 30 us -> 26.7 us
    psum x0 -> x1, blocking collectives: none -> 12.4 us  [on_device(): lax.psum(lax.psum((local_w_dt, jnp.sum(grad_pre, axis=0), jnp.sum(g_rate,...]
    psum x1, blocking collectives: 14.1 us -> 2.47 us  [on_device(): lax.psum((local_w_dt, jnp.sum(grad_pre, axis=0), jnp.sum(g_rate, axis=0)...]
    psum x1, waiting for transfers between devices: 10.8 us -> 5.25 us  [on_device(): lax.psum((local_w_dt, jnp.sum(grad_pre, axis=0), jnp.sum(g_rate, axis=0)...]
    unnamed x59 -> x57, local copies, waits for them, and re-layouts: 10.7 us -> 8.09 us
    unnamed x5 -> x6, waiting for transfers between devices: 38.5 us -> 37.2 us
  transfers between devices with their start and end apart: 4 -> 5, of which waited for: 4 -> 5; matrix products, arithmetic and copies ran while one was open for 14% -> 13% of each run, Pallas kernels for 0% -> 0%
where the time goes in v1:
time: 279 us; the launch traced here: 278 us
  waiting for transfers between devices  133 us (48%)
  blocking collectives  49.1 us (18%)
  matrix products  32.5 us (12%)
  local copies, waits for them, and re-layouts  26.7 us (10%)
  other arithmetic  21.3 us (8%)
  between operations  14.2 us (5%)
    all_gather x2, waiting for transfers between devices, prefix(): everything = jax.tree.map(lambda part: lax.all_gather(part, axis), shard)  90.5 us
    unnamed x6, waiting for transfers between devices  37.2 us
    all_gather x1, blocking collectives, prefix(): everything = jax.tree.map(lambda part: lax.all_gather(part, axis), shard)  12.8 us
    dot_general x2, matrix products, span_core(): inner = jnp.einsum('hts,shp->thp', mixing, values_in, precision=highest)  12.5 us
    psum x1, blocking collectives, on_device(): lax.psum(lax.psum((local_w_dt, jnp.sum(grad_pre, axis=0), jnp.sum(g_rate,...  12.4 us
    psum x1, blocking collectives, on_device(): grad_proj = lax.psum(partial_proj, 'head').astype(jnp.bfloat16)  11.5 us
    select_n x8, other arithmetic, turn(): return jax.tree.map(lambda a, b: jnp.where(reached, a, b), new, before)  10.4 us
    unnamed x57, local copies, waits for them, and re-layouts  8.09 us
  transfers between devices with their start and end apart: 5, of which 5 were waited for; matrix products, arithmetic and copies ran while one was open for 13% of the time, Pallas kernels for 0%

profile of v1, /device:TPU:0, one launch (start us, length us, event | category | flops | bytes accessed | tf_op | source)
XLA Modules:
  0.0 277.7 jit_solution(2344774273177045791)
XLA Ops:
  7.2 0.8 exponential_negate_fusion
  8.3 1.2 convolution_add_fusion.1
  9.6 0.7 fusion.64
  10.4 0.6 reduce-window.14
  11.7 0.4 convolution_convert_fusion
  12.3 1.8 fusion.20
  14.2 1.4 copy.91
  15.7 12.8 %all_gather.24 = f32[4,1,24]{2,1,0:T(1,128)} all-gather(f32[1,1,24]{2,1,0:T(1,128)S(1)} %get-tuple-element.387), channel_id=1, replica_groups=mesh['groups'=2,'tm'=4,'head'=2,'batch'=2] {'tm'}, dimensions={0}, use_global_device_ids=true | all-gather | bytes 480 | tf_op jit(solution)/shard_map/all_gather | solution.py:9
  28.5 52.0 %all-gather.5.cloned.1.call-done = f32[96,64,128]{2,1,0:T(8,128)} async-done(((f32[24,64,128]{2,1,0:T(8,128)}), f32[96,64,128]{2,1,0:T(8,128)}) %all-gather.5.cloned.1.call-update) | async-done | bytes 3145744 | tf_op jit(solution)/shard_map/all_gather | solution.py:9
  80.5 7.8 %while.30 = (s32[]{:T(128)}, f32[1,24,64,128]{3,2,1,0:T(8,128)S(1)}, s32[]{:T(128)}, f32[4,1,24]{2,1,0:T(1,128)}, f32[4,1,24,64,128]{4,3,2,1,0:T(8,128)}, /*index=5*/s32[]{:T(128)}, s32[]{:T(128)}, s32[]{:T(128)}, s32[]{:T(128)}) while((s32[]{:T(128)}, f32[1,24,64,128]{3,2,1,0:T(8,128)S(1)}, s32[]{:T(128)}, f32[4,1,24]{2,1,0:T(1,128)}, ...), condition=%wide.region_3.4_spmd.clone, body=%wide.region_2.3_spmd.clone.sunk | while | flops 786440 | bytes 2359751 | solution.py:22
  80.5 0.7 dynamic-slice_bitcast_fusion.4
  81.2 1.3 fusion.85
  82.5 0.6 dynamic-slice_bitcast_fusion.4
  83.1 1.3 fusion.85
  84.4 0.6 dynamic-slice_bitcast_fusion.4
  85.0 1.3 fusion.85
  86.4 0.7 dynamic-slice_bitcast_fusion.4
  87.0 1.3 fusion.85
  88.4 2.5 fusion.18
  90.9 1.5 copy.111
  92.4 2.2 fusion.61
  94.6 1.6 copy.90
  96.2 2.5 fusion.16
  98.9 1.4 copy.92
  100.3 2.0 bitcast_multiply_fusion.1
  102.3 0.7 broadcast.77
  103.0 1.6 copy.112
  104.6 1.6 copy.95
  106.2 0.8 bitcast_add_fusion.8
  107.2 6.4 %fusion.7 = (f32[24,256]{1,0:T(8,128)}, f32[24,256]{1,0:T(8,128)}, f32[24,256]{1,0:T(8,128)}, f32[256,256]{1,0:T(8,128)}) fusion(f32[256,256]{1,0:T(8,128)S(1)} %fusion.53, f32[24,256]{1,0:T(8,128)} %copy.95, f32[24,256]{1,0:T(8,128)S(1)} %bitcast_add_fusion.8, pred[256,256]{1,0:T(8,128)(4,1)S(1)} %iota_compare_fusion, ...), kind=kOutput, calls=%fused_computation.14 | convolution fusion | flops 221689856 | bytes 2285568 | tf_op jit(solution)/shard_map/vmap(transpose(jvp(hts,shp->thp)))/dot_general | solution.py:34
  113.6 1.5 copy.100
  115.1 1.5 copy.99
  116.6 1.5 copy.97
  118.0 1.2 convolution_bitcast_fusion.3
  119.3 3.3 %fusion.25 = f32[1,256,128]{1,2,0:T(8,128)} fusion(f32[1,256,128]{1,2,0:T(8,128)S(1)} %convolution_bitcast_fusion.3, bf16[256,24,64]{0,2,1:T(8,128)(2,1)} %bitcast.249, f32[1,24,64,128]{3,2,1,0:T(8,128)S(1)} %get-tuple-element.232, f32[256,24]{0,1:T(8,128)} %copy.90), kind=kOutput, calls=%fused_computation.42 | convolution fusion | flops 604798976 | bytes 1859584 | tf_op jit(solution)/shard_map/vmap(transpose(jvp(sh,shp,sn->hpn)))/dot_general | solution.py:40
  122.5 38.5 %all-gather.7.cloned.1.call-done = f32[96,64,128]{2,1,0:T(8,128)} async-done(((f32[24,64,128]{2,1,0:T(8,128)}), f32[96,64,128]{2,1,0:T(8,128)}) %all-gather.7.cloned.1.call-update) | async-done | bytes 3145744 | tf_op jit(solution)/shard_map/all_gather | solution.py:9
  161.0 7.8 %while.31 = (s32[]{:T(128)}, f32[1,24,64,128]{3,2,1,0:T(8,128)S(1)}, s32[]{:T(128)}, f32[4,1,24]{2,1,0:T(1,128)}, f32[4,1,24,64,128]{4,3,2,1,0:T(8,128)}, /*index=5*/s32[]{:T(128)}, s32[]{:T(128)}) while((s32[]{:T(128)}, f32[1,24,64,128]{3,2,1,0:T(8,128)S(1)}, s32[]{:T(128)}, f32[4,1,24]{2,1,0:T(1,128)}, ...), condition=%wide.region_6.7_spmd.clone, body=%wide.region_5.6_spmd.clone.sunk | while | flops 786436 | bytes 2359689 | solution.py:22
  161.0 0.7 dynamic-slice_bitcast_fusion.5
  161.7 1.3 fusion.86
  163.0 0.6 dynamic-slice_bitcast_fusion.5
  163.6 1.3 fusion.86
  164.9 0.6 dynamic-slice_bitcast_fusion.5
  165.5 1.3 fusion.86
  166.9 0.7 dynamic-slice_bitcast_fusion.5
  167.5 1.3 fusion.86
  169.1 0.8 multiply_reduce_fusion.2
  170.4 2.5 reduce-window.16
  173.1 2.9 %convolution_bitcast_fusion.2 = f32[256,128]{0,1:T(8,128)S(1)} fusion(f32[256,24,64]{0,2,1:T(8,128)} %bitcast.250, f32[1,24,64,128]{3,2,1,0:T(8,128)S(1)} %get-tuple-element.233), kind=kOutput, calls=%fused_computation.40 | convolution fusion | flops 603979776 | bytes 2490368 | tf_op jit(solution)/shard_map/vmap(transpose(jvp(tn,hpn->thp)))/dot_general | solution.py:35
  176.4 0.6 fusion.65
  177.0 0.9 convolution_bitcast_fusion.1
  178.0 11.5 %all-reduce.11 = bf16[256,256]{0,1:T(8,128)(2,1)S(1)} all-reduce(f32[256,256]{0,1:T(8,128)S(1)} %maximum_bitcast_fusion), channel_id=1, replica_groups=mesh['groups'=2,'tm'=4,'head'=2,'batch'=2] {'head'}, use_global_device_ids=true, to_apply=%region_7.8 | all-reduce | flops 65536 | bytes 393216 | tf_op jit(solution)/shard_map/psum | solution.py:90
  189.5 5.2 %all-reduce.8.cloned.1.call-done = f32[1536,24]{0,1:T(8,128)} async-done(((f32[1536,24]{0,1:T(8,128)}), f32[1536,24]{0,1:T(8,128)}) %all-reduce.8.cloned.1.call-update) | async-done | bytes 147472 | tf_op jit(solution)/shard_map/psum | solution.py:103
  195.2 1.6 copy.113
  196.8 5.5 %all_gather.30 = bf16[1536,48]{0,1:T(8,128)(2,1)S(1)} all-gather(bf16[1536,24]{0,1:T(8,128)(2,1)} %param.15), channel_id=1, replica_groups=mesh['groups'=2,'tm'=4,'head'=2,'batch'=2] {'head'}, dimensions={1}, use_global_device_ids=true | all-gather | bytes 221184 | tf_op jit(solution)/shard_map/all_gather | solution.py:96
  202.4 6.1 %fusion.19 = bf16[1,256,24,64]{1,3,2,0:T(8,128)(2,1)} fusion(f32[24,64,256]{2,1,0:T(8,128)S(1)} %copy-done.5, bf16[24,64,256]{2,1,0:T(8,128)(2,1)S(1)} %bitcast.245, f32[256,256]{1,0:T(8,128)} %copy-done.17, f32[24,256]{1,0:T(8,128)} %copy.95, f32[24,256]{1,0:T(8,128)} %copy-done.20, pred[256,256]{1,0:T(8,128)(4,1)} %copy-done.19, f32[256,24]{0,1:T(8,128)} %copy.90), kind=kOutput, calls=%fused_computation.32 | convolution fusion | flops 1215430656 | bytes 3547136 | tf_op jit(solution)/shard_map/vmap(transpose(jvp(hts,shp->thp)))/dot_general | solution.py:34
  208.5 2.4 copy.104
  211.1 2.5 all-reduce.3
  213.6 12.4 %all-reduce.2 = (f32[24]{0:T(128)}, f32[24]{0:T(128)}) all-reduce(f32[24]{0:T(128)S(1)} %get-tuple-element.376, f32[24]{0:T(128)S(1)} %get-tuple-element.377), channel_id=1, replica_groups=mesh['groups'=2,'tm'=4,'head'=2,'batch'=2] {'tm'}, use_global_device_ids=true, to_apply=%region_21.22 | all-reduce | flops 48 | bytes 384 | tf_op jit(solution)/shard_map/psum | solution.py:102
  226.0 4.4 %all_gather.29 = bf16[256,48]{0,1:T(8,128)(2,1)S(1)} all-gather(bf16[256,24]{0,1:T(8,128)(2,1)S(1)} %copy.103), channel_id=1, replica_groups=mesh['groups'=2,'tm'=4,'head'=2,'batch'=2] {'head'}, dimensions={1}, use_global_device_ids=true | all-gather | bytes 36864 | tf_op jit(solution)/shard_map/all_gather | solution.py:95
  230.3 0.4 fusion.68
  230.8 1.3 fusion.15
  232.0 0.4 all-reduce.10.cloned.1.call-done
  232.4 37.1 %reduce-scatter.4.cloned.1.call-done = f32[192,256]{1,0:T(8,128)} async-done(((f32[1536,256]{1,0:T(8,128)}), f32[192,256]{1,0:T(8,128)}) %reduce-scatter.4.cloned.1.call-update) | async-done | bytes 196624
  269.6 1.6 copy.133
  (90 shorter events, 3.9 us)
Async XLA Ops:
  7.2 1.2 copy-start
  7.2 4.5 %copy-start.2 = (bf16[1536,256]{1,0:T(8,128)(2,1)S(1)}, bf16[1536,256]{1,0:T(8,128)(2,1)}, u32[]{:S(2)}) copy-start(bf16[1536,256]{1,0:T(8,128)(2,1)} %param.14) | copy-start | bytes 2359300
  7.2 73.3 %all-gather.5.cloned.1.call-start = ((), (), s32[]{:S(2)}) async-start(), calls=%async_computation.3 | async-start | bytes 3932160 | tf_op jit(solution)/shard_map/all_gather | solution.py:9
  9.5 2.5 copy-start.9
  10.9 0.6 copy-start.16
  11.6 0.7 copy-start.18
  14.2 146.9 %all-gather.7.cloned.1.call-start = ((), (), s32[]{:S(2)}) async-start(), calls=%async_computation.4 | async-start | bytes 3932160 | tf_op jit(solution)/shard_map/all_gather | solution.py:9
  15.6 80.5 %copy-start.1 = (bf16[1,256,1536]{1,2,0:T(8,128)(2,1)}, bf16[1,256,1536]{1,2,0:T(8,128)(2,1)S(1)}, u32[]{:S(2)}) copy-start(bf16[1,256,1536]{1,2,0:T(8,128)(2,1)S(1)} %copy.91) | copy-start | bytes 2359300
  98.7 96.0 %all-reduce.8.cloned.1.call-start = ((), (), s32[]{:S(2)}) async-start(), calls=%async_computation.1 | async-start | bytes 294912 | tf_op jit(solution)/shard_map/psum | solution.py:103
  106.2 7.4 %copy-start.19 = (pred[256,256]{1,0:T(8,128)(4,1)}, pred[256,256]{1,0:T(8,128)(4,1)S(1)}, u32[]{:S(2)}) copy-start(pred[256,256]{1,0:T(8,128)(4,1)S(1)} %iota_compare_fusion) | copy-start | bytes 196612
  107.0 6.6 %copy-start.20 = (f32[24,256]{1,0:T(8,128)}, f32[24,256]{1,0:T(8,128)S(1)}, u32[]{:S(2)}) copy-start(f32[24,256]{1,0:T(8,128)S(1)} %bitcast_add_fusion.8) | copy-start | bytes 73732
  107.2 6.4 %copy-start.17 = (f32[256,256]{1,0:T(8,128)}, f32[256,256]{1,0:T(8,128)S(1)}, u32[]{:S(2)}) copy-start(f32[256,256]{1,0:T(8,128)S(1)} %fusion.53) | copy-start | bytes 786436
  168.8 1.2 copy-start.23
  169.1 0.9 copy-start.4
  169.1 1.0 copy-start.14
  169.1 1.0 copy-start.15
  170.3 5.8 %copy-start.8 = (f32[256,256]{1,0:T(8,128)S(1)}, f32[256,256]{1,0:T(8,128)}, u32[]{:S(2)}) copy-start(f32[256,256]{1,0:T(8,128)} %get-tuple-element.353) | copy-start | bytes 786436
  173.0 3.4 %copy-start.6 = (f32[1,24,2,128]{1,3,2,0:T(8,128)}, f32[1,24,2,128]{1,3,2,0:T(8,128)S(1)}, u32[]{:S(2)}) copy-start(f32[1,24,2,128]{1,3,2,0:T(8,128)S(1)} %copy.102) | copy-start | bytes 73732
  173.0 3.4 %copy-start.12 = (f32[1,256,128]{1,2,0:T(8,128)S(1)}, f32[1,256,128]{1,2,0:T(8,128)}, u32[]{:S(2)}) copy-start(f32[1,256,128]{1,2,0:T(8,128)} %fusion.25) | copy-start | bytes 393220
  173.1 3.3 %copy-start.21 = (f32[24,2]{0,1:T(2,128)}, f32[24,2]{0,1:T(2,128)S(1)}, u32[]{:S(2)}) copy-start(f32[24,2]{0,1:T(2,128)S(1)} %slice_bitcast_fusion) | copy-start | bytes 580
  173.1 3.3 %copy-start.13 = (f32[24,256]{0,1:T(8,128)S(1)}, f32[24,256]{0,1:T(8,128)}, u32[]{:S(2)}) copy-start(f32[24,256]{0,1:T(8,128)} %copy.97) | copy-start | bytes 73732
  177.0 0.9 copy-start.10
  178.0 54.5 %all-reduce.10.cloned.1.call-start = ((), (), s32[]{:S(2)}) async-start(), calls=%async_computation.2 | async-start | bytes 294912 | tf_op jit(solution)/shard_map/psum | solution.py:102
  194.8 74.8 %reduce-scatter.4.cloned.1.call-start = ((), (), s32[]{:S(2)}) async-start(), calls=%async_computation.5 | async-start | bytes 1769472
  196.8 5.5 %copy-start.5 = (f32[24,64,256]{2,1,0:T(8,128)S(1)}, f32[24,64,256]{2,1,0:T(8,128)}, u32[]{:S(2)}) copy-start(f32[24,64,256]{2,1,0:T(8,128)} %get-tuple-element.389) | copy-start | bytes 4718596
  208.4 2.4 copy-start.7
  208.4 2.4 copy-start.22
  208.4 2.6 copy-start.11
  208.4 2.6 copy-start.25
  208.5 2.6 copy-start.24
  208.5 21.9 %copy-start.3 = (bf16[1536,256]{1,0:T(8,128)(2,1)S(1)}, bf16[1536,256]{1,0:T(8,128)(2,1)}, u32[]{:S(2)}) copy-start(bf16[1536,256]{1,0:T(8,128)(2,1)} %param.14) | copy-start | bytes 2359300
Sparse Core Ops, SparseCore 0:
  14.3 66.1 all-gather.4
  98.8 62.1 all-gather.6
  178.1 16.6 all-reduce.7
  196.9 35.4 all-reduce.9
  235.3 34.2 reduce-scatter.3
